TPU v7x, 32 devices: a whole 2x2x4 slice. The times are simulated.
32 devices in a mesh: cp: 8 (over y, x, core), sp: 4 (over z).
Axes of the slice: x: 2, y: 2, z: 4, core: 2. Of those that a mesh axis runs over, the one named last changes fastest.
Arguments:
- queries: bfloat16 [3072, 2048], P(('cp', 'sp')), may hold values from -6 to 6
- key_vectors: bfloat16 [3072, 512], P(('cp', 'sp')), may hold values from -6 to 6
- value_matrix: bfloat16 [3072, 512], P(('cp', 'sp')), may hold values from -6 to 6
- span_order: int32 [8], replicated, may hold values from 0 to 7, each once
Outputs:
- attended: bfloat16 [3072, 2048], P(('cp', 'sp'))
Inputs may be any that keep to these rules, and one draw needn't show every extreme that they name: `span_order`: each value appears exactly once.
All inputs are finite; a program needn't handle non-finite values.
Results may differ from a plain program's by a relative error of at most 0.0055.
Values may be sent and summed in bfloat16 or wider, within the bound.
A program may use at most 128 MiB of HBM per device.

v0:
```python
import jax
import jax.numpy as jnp
from jax import lax
from jax.sharding import PartitionSpec as P

HEAD_WIDTH = 128
masked_score = -1e30


def span_position(row_ids, span_order, pair_count, span_rows):
    slot_ids = row_ids // span_rows
    pair_ids = slot_ids // 2
    picked = jnp.sum(
        jnp.where(
            pair_ids[:, None] == jnp.arange(pair_count, dtype=jnp.int32)[None, :],
            span_order[None, :],
            0,
        ),
        axis=1,
    )
    span_ids = jnp.where(slot_ids % 2 == 1, 2 * pair_count - 1 - picked, picked)
    return span_ids * span_rows + row_ids % span_rows


def absorb_block(state_in, query_blk, query_pos, key_blk, value_blk, key_pos):
    run_max, run_sum, accumulated = state_in
    scores = jnp.einsum(
        "qhd,kd->hqk", query_blk, key_blk, preferred_element_type=jnp.float32
    ) * query_blk.shape[2] ** (-0.5)
    allowed = key_pos[None, None, :] <= query_pos[None, :, None]
    new_peak = jnp.maximum(run_max, jnp.max(jnp.where(allowed, scores, masked_score), axis=2))
    weights = jnp.where(allowed, jnp.exp(scores - new_peak[:, :, None]), 0.0)
    factor = jnp.exp(run_max - new_peak)
    run_sum = run_sum * factor + jnp.sum(weights, axis=2)
    accumulated = accumulated * factor[:, :, None] + jnp.einsum(
        "hqk,kd->hqd", weights.astype(jnp.bfloat16), value_blk, preferred_element_type=jnp.float32
    )
    return (new_peak, run_sum, accumulated)


def pick_block(key_count, unit_rows):
    block_row_list = unit_rows
    while block_row_list * 2 <= 1024 and key_count % (block_row_list * 2) == 0:
        block_row_list = block_row_list * 2
    return block_row_list


def guarded(state_in, query_blk, query_pos, key_blk, value_blk, key_pos, lowest):

    def compute(states):
        return absorb_block(states, query_blk, query_pos, key_blk, value_blk, key_pos)

    def unchanged(states):
        return states

    return lax.cond(lowest <= jnp.max(query_pos), compute, unchanged, state_in)


def sweep(carries, query_list, key_rows, value_rows, position_of, block_row_list):
    key_count = key_rows.shape[0]

    def advance(states, offset):
        key_blk = lax.dynamic_slice_in_dim(key_rows, offset, block_row_list, 0)
        value_blk = lax.dynamic_slice_in_dim(value_rows, offset, block_row_list, 0)
        key_pos = position_of(offset + jnp.arange(block_row_list, dtype=jnp.int32))
        lowest = jnp.min(key_pos)
        updated = []
        for state_in, entry in zip(states, query_list):
            updated.append(
                guarded(state_in, entry[0], entry[1], key_blk, value_blk, key_pos, lowest)
            )
        return (tuple(updated), None)

    offsets = jnp.arange(key_count // block_row_list, dtype=jnp.int32) * block_row_list
    return lax.scan(advance, carries, offsets)[0]


def per_device(queries, key_vectors, value_matrix, span_order):
    tok_rows = queries.shape[0]
    cp_count = lax.axis_size("cp")
    sp_count = lax.axis_size("sp")
    local_query = lax.all_to_all(queries, "sp", split_axis=1, concat_axis=0, tiled=True)
    group_rows = local_query.shape[0]
    span_rows = group_rows // 2
    head_count = local_query.shape[1] // HEAD_WIDTH
    query_heads = local_query.reshape(group_rows, head_count, HEAD_WIDTH)
    group_id = lax.axis_index("cp")
    query_ids = group_id * group_rows + jnp.arange(group_rows, dtype=jnp.int32)
    query_pos = span_position(query_ids, span_order, cp_count, span_rows)
    query_list = [(query_heads, query_pos)]
    initial = tuple(
        (
            (
                jnp.full((head_count, entry[1].shape[0]), masked_score, jnp.float32),
                jnp.zeros((head_count, entry[1].shape[0]), jnp.float32),
                jnp.zeros((head_count, entry[1].shape[0], HEAD_WIDTH), jnp.float32),
            )
            for entry in query_list
        )
    )
    whole_key, whole_value = (
        lax.all_gather(key_vectors, "cp", axis=0, tiled=True),
        lax.all_gather(value_matrix, "cp", axis=0, tiled=True),
    )
    head_key, head_value = (
        lax.all_to_all(whole_key, "sp", split_axis=1, concat_axis=0, tiled=True),
        lax.all_to_all(whole_value, "sp", split_axis=1, concat_axis=0, tiled=True),
    )
    total_rows = head_key.shape[0]
    span_count = total_rows // span_rows
    slot_ids = jnp.arange(span_count, dtype=jnp.int32)
    pair_pick = jnp.sum(
        jnp.where(
            (slot_ids // 2)[:, None] == jnp.arange(cp_count, dtype=jnp.int32)[None, :],
            span_order[None, :],
            0,
        ),
        axis=1,
    )
    span_of_slot = jnp.where(slot_ids % 2 == 1, 2 * cp_count - 1 - pair_pick, pair_pick)
    slot_of_span = jnp.sum(
        jnp.where(span_of_slot[None, :] == slot_ids[:, None], slot_ids[None, :], 0), axis=1
    )

    def position_layout(rows):
        stored = jnp.transpose(rows.reshape(sp_count, cp_count, tok_rows, HEAD_WIDTH), (1, 0, 2, 3))
        spans = stored.reshape(span_count, span_rows, HEAD_WIDTH)
        return jnp.take(spans, slot_of_span, axis=0).reshape(total_rows, HEAD_WIDTH)

    ordered_key = position_layout(head_key)
    ordered_value = position_layout(head_value)

    def plain_position(row_ids):
        return row_ids

    carries = sweep(
        initial,
        query_list,
        ordered_key,
        ordered_value,
        plain_position,
        pick_block(total_rows, span_rows),
    )
    pieces = [entry[2] / entry[1][:, :, None] for entry in carries]
    joined = pieces[0]
    mixed_rows = (
        jnp.transpose(joined, (1, 0, 2))
        .reshape(group_rows, head_count * HEAD_WIDTH)
        .astype(jnp.bfloat16)
    )
    return lax.all_to_all(mixed_rows, "sp", split_axis=0, concat_axis=1, tiled=True)


def solution(mesh):
    return jax.shard_map(
        per_device,
        mesh=mesh,
        in_specs=(P(("cp", "sp"), None), P(("cp", "sp"), None), P(("cp", "sp"), None), P()),
        out_specs=P(("cp", "sp"), None),
        check_vma=False,
    )
```

profile of v0, /device:TPU:0, one launch (start us, length us, event | category | flops | bytes accessed | tf_op | source)
XLA Modules:
  0.0 125.0 jit_solution(15922890918576906589)
XLA Ops:
  0.0 0.0 copy-start
  0.0 0.0 copy-start.1
  0.0 1.8 %copy.54 = bf16[12,4,8,512]{3,2,0,1:T(8,128)(2,1)} copy(bf16[12,4,8,512]{3,2,1,0:T(8,128)(2,1)} %bitcast.62) | data formatting | bytes 786432 | tf_op jit(solution)/shard_map/all_to_all | solution.py:82
  1.8 6.3 %all-to-all-start.1 = ((bf16[96,4,512]{2,0,1:T(8,128)(2,1)}), bf16[96,4,512]{2,0,1:T(8,128)(2,1)S(1)}, u32[]{:S(2)}, u32[]{:S(2)}) async-start(bf16[96,4,512]{2,0,1:T(8,128)(2,1)} %bitcast.49), calls=%async_computation.1 | async-start | bytes 786432 | tf_op jit(solution)/shard_map/all_to_all | solution.py:82
  8.2 10.7 %all_gather.6 = bf16[768,512]{1,0:T(8,128)(2,1)S(1)} all-gather(bf16[96,512]{1,0:T(8,128)(2,1)} %param.11), channel_id=1, replica_groups=mesh['cp'=8,'sp'=4] {'cp'}, dimensions={0}, use_global_device_ids=true | all-gather | bytes 884736 | tf_op jit(solution)/shard_map/all_gather | solution.py:102
  18.9 1.2 copy.40
  20.1 0.0 all-to-all-done.1
  20.1 5.1 %all-to-all-start = ((bf16[768,4,128]{0,2,1:T(8,128)(2,1)}), bf16[768,4,128]{0,2,1:T(8,128)(2,1)S(1)}, u32[]{:S(2)}, u32[]{:S(2)}) async-start(bf16[768,4,128]{0,2,1:T(8,128)(2,1)} %bitcast.4), calls=%async_computation | async-start | bytes 1572864 | tf_op jit(solution)/shard_map/all_to_all | solution.py:106
  25.2 0.0 copy-done
  25.2 10.0 %all_gather.7 = bf16[768,512]{1,0:T(8,128)(2,1)S(1)} all-gather(bf16[96,512]{1,0:T(8,128)(2,1)S(1)} %copy-done), channel_id=1, replica_groups=mesh['cp'=8,'sp'=4] {'cp'}, dimensions={0}, use_global_device_ids=true | all-gather | bytes 884736 | tf_op jit(solution)/shard_map/all_gather | solution.py:103
  35.2 1.2 copy.44
  36.4 0.0 copy-done.1
  36.4 0.1 select_reduce_fusion.2
  36.5 9.3 %all-to-all-done = bf16[768,4,128]{0,2,1:T(8,128)(2,1)S(1)} async-done(((bf16[768,4,128]{0,2,1:T(8,128)(2,1)}), bf16[768,4,128]{0,2,1:T(8,128)(2,1)S(1)}, u32[]{:S(2)}, u32[]{:S(2)}) %all-to-all-start) | async-done | bytes 786464 | tf_op jit(solution)/shard_map/all_to_all | solution.py:106
  45.8 3.5 %all-to-all-start.2 = ((bf16[768,4,128]{0,2,1:T(8,128)(2,1)}), bf16[768,4,128]{0,2,1:T(8,128)(2,1)S(1)}, u32[]{:S(2)}, u32[]{:S(2)}) async-start(bf16[768,4,128]{0,2,1:T(8,128)(2,1)} %bitcast.11), calls=%async_computation.2 | async-start | bytes 1572864 | tf_op jit(solution)/shard_map/all_to_all | solution.py:107
  49.3 0.1 select_reduce_fusion.1
  49.5 0.1 select_reduce_fusion
  49.5 0.7 fusion.31
  50.3 0.1 reshape.137
  50.4 0.1 copy.47
  50.4 0.4 copy.41
  50.8 0.1 copy.42
  50.9 18.2 %all-to-all-done.2 = bf16[768,4,128]{0,2,1:T(8,128)(2,1)S(1)} async-done(((bf16[768,4,128]{0,2,1:T(8,128)(2,1)}), bf16[768,4,128]{0,2,1:T(8,128)(2,1)S(1)}, u32[]{:S(2)}, u32[]{:S(2)}) %all-to-all-start.2) | async-done | bytes 786464 | tf_op jit(solution)/shard_map/all_to_all | solution.py:107
  69.0 0.4 copy.45
  69.4 0.1 copy.46
  69.5 0.7 gather_fusion
  70.2 0.7 gather_fusion.1
  70.9 1.1 broadcast_select_fusion
  72.0 0.1 broadcast_in_dim.98
  72.1 37.8 %while.15 = (s32[]{:T(128)}, f32[4,384]{1,0:T(4,128)S(1)}, f32[4,384]{1,0:T(4,128)S(1)}, f32[4,384,128]{2,1,0:T(8,128)S(1)}, s32[4]{0:T(128)S(1)}, /*index=5*/s3...) while((s32[]{:T(128)}, f32[4,384]{1,0:T(4,128)S(1)}, ...), condition=%wide.region_10.12_spmd, body=%wide.region_4.11_spmd.sunk | while | flops 617648640 | bytes 17801024 | solution.py:75
  72.1 0.6 dynamic_slice.36
  72.6 1.2 iota_add_fusion.3
  75.1 6.4 %conditional.2 = ((f32[4,384]{1,0:T(4,128)S(1)}, f32[4,384]{1,0:T(4,128)S(1)}, f32[4,384,128]{2,1,0:T(8,128)S(1)})) conditional(s32[]{:T(128)} %convert_element_type.31, (f32[4,384]{1,0:T(4,128)S(1)}, f32[4,384]{1,0:T(4,128)S(1)}, f32[4,384,128]{2,1,0:T(8,128)S(1)}) %tuple.53, (s32[768]{0:T(1024)S(1)}, s32[384]{0:T(512)S(1)}, s32[]{:T(128)}, ...), branch_computations={%region_6.7_spmd, %region_7.10_spmd} | conditional | flops 617647104 | bytes 17797706 | solution.py:56
  76.8 0.2 broadcast_compare_fusion
  77.0 1.0 fusion
  78.0 1.0 fusion.4
  79.0 2.5 %fusion.8 = f32[4,384,128]{2,1,0:T(8,128)S(1)} fusion(f32[768,384,4]{1,0,2:T(8,128)S(1)} %get-tuple-element.282, f32[4,384]{1,0:T(4,128)S(1)} %max.5, pred[384,768]{0,1:T(8,128)(4,1)S(1)} %broadcast_compare_fusion, f32[4,384,128]{2,1,0:T(8,128)S(1)} %get-tuple-element.187, f32[4,384]{1,0:T(4,128)S(1)} %get-tuple-element.278, ...), kind=kOutput, calls=%fused_computation.11 | convolution fusion | flops 307101696 | bytes 6795268 | tf_op jit(solution)/shard_map/while/body/eval_jaxpr/cond/branch_1_fun/hqk,kd->hqd/dot_general | solution.py:35
  81.5 0.6 dynamic_slice.36
  82.1 1.2 iota_add_fusion.3
  84.5 6.4 %conditional.2 = ((f32[4,384]{1,0:T(4,128)S(1)}, f32[4,384]{1,0:T(4,128)S(1)}, f32[4,384,128]{2,1,0:T(8,128)S(1)})) conditional(s32[]{:T(128)} %convert_element_type.31, (f32[4,384]{1,0:T(4,128)S(1)}, f32[4,384]{1,0:T(4,128)S(1)}, f32[4,384,128]{2,1,0:T(8,128)S(1)}) %tuple.53, (s32[768]{0:T(1024)S(1)}, s32[384]{0:T(512)S(1)}, s32[]{:T(128)}, ...), branch_computations={%region_6.7_spmd, %region_7.10_spmd} | conditional | flops 617647104 | bytes 17797706 | solution.py:56
  86.2 0.2 broadcast_compare_fusion
  86.4 1.0 fusion
  87.4 1.0 fusion.4
  88.4 2.5 %fusion.8 = f32[4,384,128]{2,1,0:T(8,128)S(1)} fusion(f32[768,384,4]{1,0,2:T(8,128)S(1)} %get-tuple-element.282, f32[4,384]{1,0:T(4,128)S(1)} %max.5, pred[384,768]{0,1:T(8,128)(4,1)S(1)} %broadcast_compare_fusion, f32[4,384,128]{2,1,0:T(8,128)S(1)} %get-tuple-element.187, f32[4,384]{1,0:T(4,128)S(1)} %get-tuple-element.278, ...), kind=kOutput, calls=%fused_computation.11 | convolution fusion | flops 307101696 | bytes 6795268 | tf_op jit(solution)/shard_map/while/body/eval_jaxpr/cond/branch_1_fun/hqk,kd->hqd/dot_general | solution.py:35
  91.0 0.6 dynamic_slice.36
  91.5 1.2 iota_add_fusion.3
  94.0 6.4 %conditional.2 = ((f32[4,384]{1,0:T(4,128)S(1)}, f32[4,384]{1,0:T(4,128)S(1)}, f32[4,384,128]{2,1,0:T(8,128)S(1)})) conditional(s32[]{:T(128)} %convert_element_type.31, (f32[4,384]{1,0:T(4,128)S(1)}, f32[4,384]{1,0:T(4,128)S(1)}, f32[4,384,128]{2,1,0:T(8,128)S(1)}) %tuple.53, (s32[768]{0:T(1024)S(1)}, s32[384]{0:T(512)S(1)}, s32[]{:T(128)}, ...), branch_computations={%region_6.7_spmd, %region_7.10_spmd} | conditional | flops 617647104 | bytes 17797706 | solution.py:56
  95.6 0.2 broadcast_compare_fusion
  95.9 1.0 fusion
  96.9 1.0 fusion.4
  97.9 2.5 %fusion.8 = f32[4,384,128]{2,1,0:T(8,128)S(1)} fusion(f32[768,384,4]{1,0,2:T(8,128)S(1)} %get-tuple-element.282, f32[4,384]{1,0:T(4,128)S(1)} %max.5, pred[384,768]{0,1:T(8,128)(4,1)S(1)} %broadcast_compare_fusion, f32[4,384,128]{2,1,0:T(8,128)S(1)} %get-tuple-element.187, f32[4,384]{1,0:T(4,128)S(1)} %get-tuple-element.278, ...), kind=kOutput, calls=%fused_computation.11 | convolution fusion | flops 307101696 | bytes 6795268 | tf_op jit(solution)/shard_map/while/body/eval_jaxpr/cond/branch_1_fun/hqk,kd->hqd/dot_general | solution.py:35
  100.4 0.6 dynamic_slice.36
  101.0 1.2 iota_add_fusion.3
  103.4 6.4 %conditional.2 = ((f32[4,384]{1,0:T(4,128)S(1)}, f32[4,384]{1,0:T(4,128)S(1)}, f32[4,384,128]{2,1,0:T(8,128)S(1)})) conditional(s32[]{:T(128)} %convert_element_type.31, (f32[4,384]{1,0:T(4,128)S(1)}, f32[4,384]{1,0:T(4,128)S(1)}, f32[4,384,128]{2,1,0:T(8,128)S(1)}) %tuple.53, (s32[768]{0:T(1024)S(1)}, s32[384]{0:T(512)S(1)}, s32[]{:T(128)}, ...), branch_computations={%region_6.7_spmd, %region_7.10_spmd} | conditional | flops 617647104 | bytes 17797706 | solution.py:56
  105.1 0.2 broadcast_compare_fusion
  105.3 1.0 fusion
  106.3 1.0 fusion.4
  107.3 2.5 %fusion.8 = f32[4,384,128]{2,1,0:T(8,128)S(1)} fusion(f32[768,384,4]{1,0,2:T(8,128)S(1)} %get-tuple-element.282, f32[4,384]{1,0:T(4,128)S(1)} %max.5, pred[384,768]{0,1:T(8,128)(4,1)S(1)} %broadcast_compare_fusion, f32[4,384,128]{2,1,0:T(8,128)S(1)} %get-tuple-element.187, f32[4,384]{1,0:T(4,128)S(1)} %get-tuple-element.278, ...), kind=kOutput, calls=%fused_computation.11 | convolution fusion | flops 307101696 | bytes 6795268 | tf_op jit(solution)/shard_map/while/body/eval_jaxpr/cond/branch_1_fun/hqk,kd->hqd/dot_general | solution.py:35
  109.8 0.3 fusion.21
  110.1 0.3 copy.48
  110.4 0.2 convert_element_type.22
  110.6 13.6 %all_to_all.64 = bf16[4,96,512]{2,1,0:T(8,128)(2,1)S(1)} all-to-all(bf16[4,96,512]{2,1,0:T(8,128)(2,1)S(1)} %convert_element_type.22), channel_id=1, replica_groups=mesh['cp'=8,'sp'=4] {'sp'}, dimensions={0} | all-to-all | bytes 786432 | tf_op jit(solution)/shard_map/all_to_all | solution.py:151
  124.2 0.8 copy.52
  (21 shorter events, 0.2 us)
Async XLA Ops:
  0.0 25.2 %copy-start = (bf16[96,512]{1,0:T(8,128)(2,1)S(1)}, bf16[96,512]{1,0:T(8,128)(2,1)}, u32[]{:S(2)}) copy-start(bf16[96,512]{1,0:T(8,128)(2,1)} %param.12) | copy-start | bytes 294916
  0.0 36.4 %copy-start.1 = (s32[8]{0:T(128)S(1)}, s32[8]{0:T(128)}, u32[]{:S(2)}) copy-start(s32[8]{0:T(128)} %param.13) | copy-start | bytes 100
  1.8 18.3 %all-to-all-start.1 = ((bf16[96,4,512]{2,0,1:T(8,128)(2,1)}), bf16[96,4,512]{2,0,1:T(8,128)(2,1)S(1)}, u32[]{:S(2)}, u32[]{:S(2)}) async-start(bf16[96,4,512]{2,0,1:T(8,128)(2,1)} %bitcast.49), calls=%async_computation.1 | async-start | bytes 786432 | tf_op jit(solution)/shard_map/all_to_all | solution.py:82
  20.1 25.7 %all-to-all-start = ((bf16[768,4,128]{0,2,1:T(8,128)(2,1)}), bf16[768,4,128]{0,2,1:T(8,128)(2,1)S(1)}, u32[]{:S(2)}, u32[]{:S(2)}) async-start(bf16[768,4,128]{0,2,1:T(8,128)(2,1)} %bitcast.4), calls=%async_computation | async-start | bytes 1572864 | tf_op jit(solution)/shard_map/all_to_all | solution.py:106
  45.8 23.2 %all-to-all-start.2 = ((bf16[768,4,128]{0,2,1:T(8,128)(2,1)}), bf16[768,4,128]{0,2,1:T(8,128)(2,1)S(1)}, u32[]{:S(2)}, u32[]{:S(2)}) async-start(bf16[768,4,128]{0,2,1:T(8,128)(2,1)} %bitcast.11), calls=%async_computation.2 | async-start | bytes 1572864 | tf_op jit(solution)/shard_map/all_to_all | solution.py:107
where the time goes:
time: 126 us; the launch traced here: 125 us
  blocking collectives  34.4 us (27%)
  waiting for transfers between devices  27.5 us (22%)
  starting transfers between devices  14.9 us (12%)
  matrix products  13.7 us (11%)
  other arithmetic  12.2 us (10%)
  loops' own time  12 us (10%)
  local copies, waits for them, and re-layouts  10.1 us (8%)
    all_to_all x1, waiting for transfers between devices, per_device(): lax.all_to_all(whole_value, 'sp', split_axis=1, concat_axis=0, tiled=True)  18.2 us
    all_to_all x1, blocking collectives, per_device(): lax.all_to_all(mixed_rows, 'sp', split_axis=0, concat_axis=1, tiled=True)  13.6 us
    all_gather x1, blocking collectives, per_device(): lax.all_gather(key_vectors, 'cp', axis=0, tiled=True)  10.7 us
    all_gather x1, blocking collectives, per_device(): lax.all_gather(value_matrix, 'cp', axis=0, tiled=True)  10 us
    dot_general x4, matrix products, absorb_block(): jnp.einsum('hqk,kd->hqd', weights.astype(jnp.bfloat16), value_blk, prefer...  9.88 us
    all_to_all x1, waiting for transfers between devices, per_device(): lax.all_to_all(whole_key, 'sp', split_axis=1, concat_axis=0, tiled=True)  9.34 us
    another operation x4, loops' own time, guarded(): return lax.cond(lowest <= jnp.max(query_pos), compute, unchanged, state_in)  6.78 us
    all_to_all x1, starting transfers between devices, per_device(): lax.all_to_all(queries, 'sp', split_axis=1, concat_axis=0, tiled=True)  6.35 us
  transfers between devices with their start and end apart: 3, of which 2 were waited for; matrix products, arithmetic and copies ran while one was open for 3% of the time, Pallas kernels for 0%

commit v1 on v0

--- a/solution.py
+++ b/solution.py
@@ -104,7 +104,12 @@
     )
     head_key, head_value = (
         lax.all_to_all(whole_key, "sp", split_axis=1, concat_axis=0, tiled=True),
-        lax.all_to_all(whole_value, "sp", split_axis=1, concat_axis=0, tiled=True),
+        jnp.concatenate(
+            lax.all_to_all(
+                jnp.stack(jnp.split(whole_value, lax.axis_size("sp"), axis=1)), "sp", 0, 0
+            ),
+            axis=0,
+        ),
     )
     total_rows = head_key.shape[0]
     span_count = total_rows // span_rows

time: 126 us -> 123 us (0.976)
  matrix products: 13.7 us -> 10.1 us
  loops' own time: 12 us -> 13.4 us
    dot_general x4, matrix products: 9.88 us -> 6.25 us  [absorb_block(): jnp.einsum('hqk,kd->hqd', weights.astype(jnp.bfloat16), value_blk, prefer...]
    another operation x4, loops' own time: 6.78 us -> 8.48 us  [guarded(): return lax.cond(lowest <= jnp.max(query_pos), compute, unchanged, state_in)]
where the time goes in v1:
time: 123 us; the launch traced here: 122 us
  blocking collectives  34.4 us (28%)
  waiting for transfers between devices  27.5 us (22%)
  starting transfers between devices  14.9 us (12%)
  loops' own time  13.4 us (11%)
  other arithmetic  12.8 us (10%)
  matrix products  10.1 us (8%)
  local copies, waits for them, and re-layouts  9.14 us (7%)
    all_to_all x1, waiting for transfers between devices, per_device(): lax.all_to_all(jnp.stack(jnp.split(whole_value, lax.axis_size('sp'), axis...  18.2 us
    all_to_all x1, blocking collectives, per_device(): lax.all_to_all(mixed_rows, 'sp', split_axis=0, concat_axis=1, tiled=True)  13.6 us
    all_gather x1, blocking collectives, per_device(): lax.all_gather(key_vectors, 'cp', axis=0, tiled=True)  10.7 us
    all_gather x1, blocking collectives, per_device(): lax.all_gather(value_matrix, 'cp', axis=0, tiled=True)  10 us
    all_to_all x1, waiting for transfers between devices, per_device(): lax.all_to_all(whole_key, 'sp', split_axis=1, concat_axis=0, tiled=True)  9.37 us
    another operation x4, loops' own time, guarded(): return lax.cond(lowest <= jnp.max(query_pos), compute, unchanged, state_in)  8.48 us
    all_to_all x1, starting transfers between devices, per_device(): lax.all_to_all(queries, 'sp', split_axis=1, concat_axis=0, tiled=True)  6.35 us
    dot_general x4, matrix products, absorb_block(): jnp.einsum('hqk,kd->hqd', weights.astype(jnp.bfloat16), value_blk, prefer...  6.25 us
  transfers between devices with their start and end apart: 3, of which 2 were waited for; matrix products, arithmetic and copies ran while one was open for 3% of the time, Pallas kernels for 0%

profile of v1, /device:TPU:0, one launch (start us, length us, event | category | flops | bytes accessed | tf_op | source)
XLA Modules:
  0.0 122.4 jit_solution(5827007886364631387)
XLA Ops:
  0.0 0.0 copy-start.1
  0.0 0.0 copy-start
  0.0 1.8 %copy.48 = bf16[12,4,8,512]{3,2,0,1:T(8,128)(2,1)} copy(bf16[12,4,8,512]{3,2,1,0:T(8,128)(2,1)} %bitcast.67) | data formatting | bytes 786432 | tf_op jit(solution)/shard_map/all_to_all | solution.py:82
  1.8 6.3 %all-to-all-start.1 = ((bf16[96,4,512]{2,0,1:T(8,128)(2,1)}), bf16[96,4,512]{2,0,1:T(8,128)(2,1)S(1)}, u32[]{:S(2)}, u32[]{:S(2)}) async-start(bf16[96,4,512]{2,0,1:T(8,128)(2,1)} %bitcast.55), calls=%async_computation.1 | async-start | bytes 786432 | tf_op jit(solution)/shard_map/all_to_all | solution.py:82
  8.2 10.7 %all_gather.6 = bf16[768,512]{1,0:T(8,128)(2,1)S(1)} all-gather(bf16[96,512]{1,0:T(8,128)(2,1)} %param.11), channel_id=1, replica_groups=mesh['cp'=8,'sp'=4] {'cp'}, dimensions={0}, use_global_device_ids=true | all-gather | bytes 884736 | tf_op jit(solution)/shard_map/all_gather | solution.py:102
  18.9 1.2 copy.36
  20.1 0.0 all-to-all-done.1
  20.1 5.1 %all-to-all-start = ((bf16[768,4,128]{0,2,1:T(8,128)(2,1)}), bf16[768,4,128]{0,2,1:T(8,128)(2,1)S(1)}, u32[]{:S(2)}, u32[]{:S(2)}) async-start(bf16[768,4,128]{0,2,1:T(8,128)(2,1)} %bitcast.4), calls=%async_computation | async-start | bytes 1572864 | tf_op jit(solution)/shard_map/all_to_all | solution.py:106
  25.2 0.0 copy-done.1
  25.2 0.1 select_reduce_fusion.2
  25.3 0.0 copy-done
  25.3 10.0 %all_gather.7 = bf16[768,512]{1,0:T(8,128)(2,1)S(1)} all-gather(bf16[96,512]{1,0:T(8,128)(2,1)S(1)} %copy-done), channel_id=1, replica_groups=mesh['cp'=8,'sp'=4] {'cp'}, dimensions={0}, use_global_device_ids=true | all-gather | bytes 884736 | tf_op jit(solution)/shard_map/all_gather | solution.py:103
  35.3 0.1 slice_bitcast_fusion.3
  35.5 1.0 pad_maximum_fusion
  36.4 9.4 %all-to-all-done = bf16[768,4,128]{0,2,1:T(8,128)(2,1)S(1)} async-done(((bf16[768,4,128]{0,2,1:T(8,128)(2,1)}), bf16[768,4,128]{0,2,1:T(8,128)(2,1)S(1)}, u32[]{:S(2)}, u32[]{:S(2)}) %all-to-all-start) | async-done | bytes 786464 | tf_op jit(solution)/shard_map/all_to_all | solution.py:106
  45.8 3.5 %all-to-all-start.2 = ((bf16[4,768,128]{2,1,0:T(8,128)(2,1)}), bf16[4,768,128]{2,1,0:T(8,128)(2,1)S(1)}, u32[]{:S(2)}, u32[]{:S(2)}) async-start(bf16[4,768,128]{2,1,0:T(8,128)(2,1)} %pad_maximum_fusion), calls=%async_computation.2 | async-start | bytes 1572864 | tf_op jit(solution)/shard_map/all_to_all | solution.py:108
  49.3 0.1 select_reduce_fusion.1
  49.5 0.1 select_reduce_fusion
  49.5 0.7 fusion.31
  50.3 0.1 reshape.130
  50.4 0.1 copy.41
  50.4 0.4 copy.37
  50.8 0.1 copy.38
  50.9 18.2 %all-to-all-done.2 = bf16[4,768,128]{2,1,0:T(8,128)(2,1)S(1)} async-done(((bf16[4,768,128]{2,1,0:T(8,128)(2,1)}), bf16[4,768,128]{2,1,0:T(8,128)(2,1)S(1)}, u32[]{:S(2)}, u32[]{:S(2)}) %all-to-all-start.2) | async-done | bytes 786464 | tf_op jit(solution)/shard_map/all_to_all | solution.py:108
  69.0 0.1 copy.40
  69.1 0.7 gather_fusion
  69.8 0.7 gather_fusion.1
  70.5 0.2 broadcast_select_fusion
  70.8 0.1 broadcast_in_dim.98
  70.8 36.4 %while.15 = (s32[]{:T(128)}, f32[4,384]{1,0:T(4,128)S(1)}, f32[4,384]{1,0:T(4,128)S(1)}, f32[4,384,128]{2,1,0:T(8,128)S(1)}, s32[4]{0:T(128)S(1)}, /*index=5*/s3...) while((s32[]{:T(128)}, f32[4,384]{1,0:T(4,128)S(1)}, ...), condition=%wide.region_10.12_spmd, body=%wide.region_4.11_spmd.sunk | while | flops 617648640 | bytes 17801024 | solution.py:75
  70.8 0.7 dynamic_slice.36
  71.5 1.3 %iota_add_fusion.3 = (s32[768]{0:T(1024)S(1)}, s32[]{:T(128)}) fusion(s32[]{:T(128)} %bitcast.57), kind=kLoop, calls=%fused_computation.24.clone.2 | loop fusion | flops 1535 | bytes 3080 | tf_op jit(solution)/shard_map/while/body/eval_jaxpr/add | solution.py:65
  74.0 5.9 %conditional.2 = ((f32[4,384]{1,0:T(4,128)S(1)}, f32[4,384]{1,0:T(4,128)S(1)}, f32[4,384,128]{2,1,0:T(8,128)S(1)})) conditional(s32[]{:T(128)} %convert_element_type.31, (f32[4,384]{1,0:T(4,128)S(1)}, f32[4,384]{1,0:T(4,128)S(1)}, f32[4,384,128]{2,1,0:T(8,128)S(1)}) %tuple.56, (s32[768]{0:T(1024)S(1)}, s32[384]{0:T(512)S(1)}, s32[]{:T(128)}, ...), branch_computations={%region_6.7_spmd, %region_7.10_spmd} | conditional | flops 617647104 | bytes 17797706 | solution.py:56
  76.1 0.2 broadcast_compare_fusion
  76.3 1.0 fusion
  77.3 1.0 fusion.4
  78.3 1.6 %fusion.8 = f32[4,384,128]{2,1,0:T(8,128)S(1)} fusion(f32[768,384,4]{1,0,2:T(8,128)S(1)} %get-tuple-element.282, f32[4,384]{1,0:T(4,128)S(1)} %max.5, pred[384,768]{0,1:T(8,128)(4,1)S(1)} %broadcast_compare_fusion, f32[4,384,128]{2,1,0:T(8,128)S(1)} %get-tuple-element.187, f32[4,384]{1,0:T(4,128)S(1)} %get-tuple-element.278, ...), kind=kOutput, calls=%fused_computation.11 | convolution fusion | flops 307101696 | bytes 6795268 | tf_op jit(solution)/shard_map/while/body/eval_jaxpr/cond/branch_1_fun/hqk,kd->hqd/dot_general | solution.py:35
  79.9 0.7 dynamic_slice.36
  80.6 1.3 %iota_add_fusion.3 = (s32[768]{0:T(1024)S(1)}, s32[]{:T(128)}) fusion(s32[]{:T(128)} %bitcast.57), kind=kLoop, calls=%fused_computation.24.clone.2 | loop fusion | flops 1535 | bytes 3080 | tf_op jit(solution)/shard_map/while/body/eval_jaxpr/add | solution.py:65
  83.1 5.9 %conditional.2 = ((f32[4,384]{1,0:T(4,128)S(1)}, f32[4,384]{1,0:T(4,128)S(1)}, f32[4,384,128]{2,1,0:T(8,128)S(1)})) conditional(s32[]{:T(128)} %convert_element_type.31, (f32[4,384]{1,0:T(4,128)S(1)}, f32[4,384]{1,0:T(4,128)S(1)}, f32[4,384,128]{2,1,0:T(8,128)S(1)}) %tuple.56, (s32[768]{0:T(1024)S(1)}, s32[384]{0:T(512)S(1)}, s32[]{:T(128)}, ...), branch_computations={%region_6.7_spmd, %region_7.10_spmd} | conditional | flops 617647104 | bytes 17797706 | solution.py:56
  85.2 0.2 broadcast_compare_fusion
  85.4 1.0 fusion
  86.4 1.0 fusion.4
  87.4 1.6 %fusion.8 = f32[4,384,128]{2,1,0:T(8,128)S(1)} fusion(f32[768,384,4]{1,0,2:T(8,128)S(1)} %get-tuple-element.282, f32[4,384]{1,0:T(4,128)S(1)} %max.5, pred[384,768]{0,1:T(8,128)(4,1)S(1)} %broadcast_compare_fusion, f32[4,384,128]{2,1,0:T(8,128)S(1)} %get-tuple-element.187, f32[4,384]{1,0:T(4,128)S(1)} %get-tuple-element.278, ...), kind=kOutput, calls=%fused_computation.11 | convolution fusion | flops 307101696 | bytes 6795268 | tf_op jit(solution)/shard_map/while/body/eval_jaxpr/cond/branch_1_fun/hqk,kd->hqd/dot_general | solution.py:35
  89.0 0.7 dynamic_slice.36
  89.7 1.3 %iota_add_fusion.3 = (s32[768]{0:T(1024)S(1)}, s32[]{:T(128)}) fusion(s32[]{:T(128)} %bitcast.57), kind=kLoop, calls=%fused_computation.24.clone.2 | loop fusion | flops 1535 | bytes 3080 | tf_op jit(solution)/shard_map/while/body/eval_jaxpr/add | solution.py:65
  92.2 5.9 %conditional.2 = ((f32[4,384]{1,0:T(4,128)S(1)}, f32[4,384]{1,0:T(4,128)S(1)}, f32[4,384,128]{2,1,0:T(8,128)S(1)})) conditional(s32[]{:T(128)} %convert_element_type.31, (f32[4,384]{1,0:T(4,128)S(1)}, f32[4,384]{1,0:T(4,128)S(1)}, f32[4,384,128]{2,1,0:T(8,128)S(1)}) %tuple.56, (s32[768]{0:T(1024)S(1)}, s32[384]{0:T(512)S(1)}, s32[]{:T(128)}, ...), branch_computations={%region_6.7_spmd, %region_7.10_spmd} | conditional | flops 617647104 | bytes 17797706 | solution.py:56
  94.3 0.2 broadcast_compare_fusion
  94.5 1.0 fusion
  95.5 1.0 fusion.4
  96.6 1.6 %fusion.8 = f32[4,384,128]{2,1,0:T(8,128)S(1)} fusion(f32[768,384,4]{1,0,2:T(8,128)S(1)} %get-tuple-element.282, f32[4,384]{1,0:T(4,128)S(1)} %max.5, pred[384,768]{0,1:T(8,128)(4,1)S(1)} %broadcast_compare_fusion, f32[4,384,128]{2,1,0:T(8,128)S(1)} %get-tuple-element.187, f32[4,384]{1,0:T(4,128)S(1)} %get-tuple-element.278, ...), kind=kOutput, calls=%fused_computation.11 | convolution fusion | flops 307101696 | bytes 6795268 | tf_op jit(solution)/shard_map/while/body/eval_jaxpr/cond/branch_1_fun/hqk,kd->hqd/dot_general | solution.py:35
  98.2 0.7 dynamic_slice.36
  98.8 1.3 %iota_add_fusion.3 = (s32[768]{0:T(1024)S(1)}, s32[]{:T(128)}) fusion(s32[]{:T(128)} %bitcast.57), kind=kLoop, calls=%fused_computation.24.clone.2 | loop fusion | flops 1535 | bytes 3080 | tf_op jit(solution)/shard_map/while/body/eval_jaxpr/add | solution.py:65
  101.3 5.9 %conditional.2 = ((f32[4,384]{1,0:T(4,128)S(1)}, f32[4,384]{1,0:T(4,128)S(1)}, f32[4,384,128]{2,1,0:T(8,128)S(1)})) conditional(s32[]{:T(128)} %convert_element_type.31, (f32[4,384]{1,0:T(4,128)S(1)}, f32[4,384]{1,0:T(4,128)S(1)}, f32[4,384,128]{2,1,0:T(8,128)S(1)}) %tuple.56, (s32[768]{0:T(1024)S(1)}, s32[384]{0:T(512)S(1)}, s32[]{:T(128)}, ...), branch_computations={%region_6.7_spmd, %region_7.10_spmd} | conditional | flops 617647104 | bytes 17797706 | solution.py:56
  103.4 0.2 broadcast_compare_fusion
  103.6 1.0 fusion
  104.6 1.0 fusion.4
  105.7 1.6 %fusion.8 = f32[4,384,128]{2,1,0:T(8,128)S(1)} fusion(f32[768,384,4]{1,0,2:T(8,128)S(1)} %get-tuple-element.282, f32[4,384]{1,0:T(4,128)S(1)} %max.5, pred[384,768]{0,1:T(8,128)(4,1)S(1)} %broadcast_compare_fusion, f32[4,384,128]{2,1,0:T(8,128)S(1)} %get-tuple-element.187, f32[4,384]{1,0:T(4,128)S(1)} %get-tuple-element.278, ...), kind=kOutput, calls=%fused_computation.11 | convolution fusion | flops 307101696 | bytes 6795268 | tf_op jit(solution)/shard_map/while/body/eval_jaxpr/cond/branch_1_fun/hqk,kd->hqd/dot_general | solution.py:35
  107.2 0.3 fusion.21
  107.5 0.3 copy.42
  107.8 0.2 convert_element_type.22
  108.0 13.6 %all_to_all.53 = bf16[4,96,512]{2,1,0:T(8,128)(2,1)S(1)} all-to-all(bf16[4,96,512]{2,1,0:T(8,128)(2,1)S(1)} %convert_element_type.22), channel_id=1, replica_groups=mesh['cp'=8,'sp'=4] {'sp'}, dimensions={0} | all-to-all | bytes 786432 | tf_op jit(solution)/shard_map/all_to_all | solution.py:156
  121.6 0.8 copy.46
  (21 shorter events, 0.2 us)
Async XLA Ops:
  0.0 25.2 %copy-start.1 = (s32[8]{0:T(128)S(1)}, s32[8]{0:T(128)}, u32[]{:S(2)}) copy-start(s32[8]{0:T(128)} %param.13) | copy-start | bytes 100
  0.0 25.3 %copy-start = (bf16[96,512]{1,0:T(8,128)(2,1)S(1)}, bf16[96,512]{1,0:T(8,128)(2,1)}, u32[]{:S(2)}) copy-start(bf16[96,512]{1,0:T(8,128)(2,1)} %param.12) | copy-start | bytes 294916
  1.8 18.3 %all-to-all-start.1 = ((bf16[96,4,512]{2,0,1:T(8,128)(2,1)}), bf16[96,4,512]{2,0,1:T(8,128)(2,1)S(1)}, u32[]{:S(2)}, u32[]{:S(2)}) async-start(bf16[96,4,512]{2,0,1:T(8,128)(2,1)} %bitcast.55), calls=%async_computation.1 | async-start | bytes 786432 | tf_op jit(solution)/shard_map/all_to_all | solution.py:82
  20.1 25.7 %all-to-all-start = ((bf16[768,4,128]{0,2,1:T(8,128)(2,1)}), bf16[768,4,128]{0,2,1:T(8,128)(2,1)S(1)}, u32[]{:S(2)}, u32[]{:S(2)}) async-start(bf16[768,4,128]{0,2,1:T(8,128)(2,1)} %bitcast.4), calls=%async_computation | async-start | bytes 1572864 | tf_op jit(solution)/shard_map/all_to_all | solution.py:106
  45.8 23.2 %all-to-all-start.2 = ((bf16[4,768,128]{2,1,0:T(8,128)(2,1)}), bf16[4,768,128]{2,1,0:T(8,128)(2,1)S(1)}, u32[]{:S(2)}, u32[]{:S(2)}) async-start(bf16[4,768,128]{2,1,0:T(8,128)(2,1)} %pad_maximum_fusion), calls=%async_computation.2 | async-start | bytes 1572864 | tf_op jit(solution)/shard_map/all_to_all | solution.py:108
